TPU v7x, 32 devices: a whole 2x2x4 slice. The times are simulated.
32 devices in a mesh: ctx: 16 (over z, y, core), head: 2 (over x).
Axes of the slice: x: 2, y: 2, z: 4, core: 2. Of those that a mesh axis runs over, the one named last changes fastest.
Arguments:
- queries: bfloat16 [2048, 8192], P('ctx', 'head'), may hold values from -5.5 to 5.5
- keys: bfloat16 [2048, 1024], P('ctx', 'head'), may hold values from -5.5 to 5.5
- values: bfloat16 [2048, 1024], P('ctx', 'head'), may hold values from -6 to 6
- feature_weights: bfloat16 [64, 128, 64], P('head'), may hold values from -1 to 1
Outputs:
- attn_error: float32 [2048, 8192], P('ctx', 'head')
- loss: float32 [], replicated
- grad_w: float32 [64, 128, 64], P('head')
All inputs are finite; a program needn't handle non-finite values.
Results may differ from a plain program's by a relative error of at most 0.004.
Values may be sent and summed in bfloat16 or wider, within the bound.
No kernel may reach another device: no remote copies, remote signals or barrier semaphores. Data moves between devices by JAX's collectives and lax.ppermute only.
A program may use at most 192 MiB of HBM per device.

v0:
```python
import math
import jax
import jax.numpy as jnp
from jax import lax
from jax.sharding import PartitionSpec as P

HEAD_SIZE = 128
QUERY_HEADS = 64
KEY_VALUE_HEADS = 8
FM = 64
WIN = 64
phi_scale = 0.00390625
big_negative = -1e30
highest = lax.Precision.HIGHEST


def swapped(value, axis, distance):
    mask = 2**distance
    pairs = [(source, source ^ mask) for source in range(lax.axis_size(axis))]
    return lax.ppermute(value, axis, pairs)


def carried_in(value, axis, combine, identity):
    devices, here = (lax.axis_size(axis), lax.axis_index(axis))
    everything = jax.tree.map(
        lambda part, kind: lax.all_gather(part.astype(kind), axis),
        value,
        (jnp.bfloat16, jnp.bfloat16),
    )
    start = jax.tree.map(
        lambda part, zero: jnp.broadcast_to(jnp.asarray(zero, part.dtype), part.shape),
        value,
        identity,
    )

    def carried_step(k, before):
        reached = k < here
        new = combine(
            before, jax.tree.map(lambda part, own: part[k].astype(own.dtype), everything, value)
        )
        return jax.tree.map(lambda a, b: jnp.where(reached, a, b), new, before)

    return lax.fori_loop(0, devices, carried_step, start)


def prefix(value, axis, combine, identity):
    devices, here = (lax.axis_size(axis), lax.axis_index(axis))
    everything = jax.tree.map(
        lambda part, kind: lax.all_gather(part.astype(kind), axis),
        value,
        jax.tree.map(lambda a: jnp.bfloat16 if a.dtype == jnp.float32 else a.dtype, value),
    )
    start = jax.tree.map(
        lambda part, zero: jnp.broadcast_to(jnp.asarray(zero, part.dtype), part.shape),
        value,
        identity,
    )

    def prefix_step(k, before):
        at = devices - 1 - k
        reached = at > here
        new = combine(
            before, jax.tree.map(lambda part, own: part[at].astype(own.dtype), everything, value)
        )
        return jax.tree.map(lambda a, b: jnp.where(reached, a, b), new, before)

    return lax.fori_loop(0, devices, prefix_step, start)


def features(projection):
    return phi_scale * jnp.concatenate(
        [1.0 + jax.nn.elu(projection), 1.0 + jax.nn.elu(-projection)], axis=-1
    )


def feature_back(projection, grad_phi):
    half = projection.shape[-1]
    slope_plus = jnp.where(projection > 0, 1.0, jnp.exp(jnp.minimum(projection, 0.0)))
    slope_minus = jnp.where(projection < 0, 1.0, jnp.exp(jnp.minimum(-projection, 0.0)))
    return phi_scale * (grad_phi[..., :half] * slope_plus - grad_phi[..., half:] * slope_minus)


def add_pair(earlier, later):
    return (earlier[0] + later[0], earlier[1] + later[1])


def split_product(form, phi_part, data):
    upper = phi_part.astype(jnp.bfloat16)
    lower = (phi_part - upper.astype(jnp.float32)).astype(jnp.bfloat16)
    return jnp.einsum(form, upper, data, preferred_element_type=jnp.float32) + jnp.einsum(
        form, lower, data, preferred_element_type=jnp.float32
    )


def visit_partner(rows):
    for bit_index in range(lax.axis_size("ctx").bit_length() - 1):
        rows = swapped(rows, "ctx", bit_index)
    return rows


def return_partner(rows):
    for bit_index in range(lax.axis_size("ctx").bit_length() - 1):
        rows = swapped(rows.astype(jnp.bfloat16), "ctx", bit_index).astype(rows.dtype)
    return rows


def teacher_part(part, query_set, pos_set, key_block, value_block, key_pos, masked):
    scale_factor = 1.0 / math.sqrt(query_set.shape[-1])
    scores = (
        jnp.einsum("qgrd,kgd->grqk", query_set, key_block, preferred_element_type=jnp.float32)
        * scale_factor
    )
    if masked:
        causal = key_pos[None, :] <= pos_set[:, None]
        top = jnp.maximum(part[0], jnp.max(jnp.where(causal, scores, big_negative), axis=-1))
        weights = jnp.exp(jnp.where(causal, scores - top[..., None], big_negative))
    else:
        top = jnp.maximum(part[0], jnp.max(scores, axis=-1))
        weights = jnp.exp(scores - top[..., None])
    rescale = jnp.exp(part[0] - top)
    total = part[1] * rescale + jnp.sum(weights, axis=-1)
    mixed = part[2] * rescale[..., None] + jnp.einsum(
        "grqk,kgd->grqd",
        weights.astype(jnp.bfloat16),
        value_block,
        preferred_element_type=jnp.float32,
    )
    return (top, total, mixed)


def advance(part, row_set, key_block, value_block, key_pos, first):
    query_set, pos_set = row_set
    needed = first <= pos_set[-1]
    straddle = key_pos[-1] > pos_set[0]
    branch_index = jnp.where(needed, jnp.where(straddle, 2, 1), 0).astype(jnp.int32)
    return lax.switch(
        branch_index,
        [
            lambda current: current,
            lambda current: teacher_part(
                current, query_set, pos_set, key_block, value_block, key_pos, False
            ),
            lambda current: teacher_part(
                current, query_set, pos_set, key_block, value_block, key_pos, True
            ),
        ],
        part,
    )


def shards(queries, keys, values, feature_weights):
    local_rows = queries.shape[0]
    half_rows = local_rows // 2
    groups = keys.shape[1] // HEAD_SIZE
    group_ratio = QUERY_HEADS // KEY_VALUE_HEADS
    heads_here = groups * group_ratio
    ctx_count = lax.axis_size("ctx")
    ctx_place = lax.axis_index("ctx")
    own_start = ctx_place * local_rows
    query4 = queries.reshape(local_rows, groups, group_ratio, HEAD_SIZE)
    own_keys = keys.reshape(local_rows, groups, HEAD_SIZE)
    own_values = values.reshape(local_rows, groups, HEAD_SIZE)
    weight4 = feature_weights.reshape(groups, group_ratio, HEAD_SIZE, FM)
    scale = 1.0 / math.sqrt(HEAD_SIZE)
    query_pos = own_start + jnp.arange(local_rows, dtype=jnp.int32)
    tail_offsets = jnp.arange(WIN, dtype=jnp.int32)
    proj_own = jnp.einsum("kgd,grdf->grkf", own_keys, weight4, preferred_element_type=jnp.float32)
    first_set = (query4[:half_rows], query_pos[:half_rows])
    partner_start = (ctx_count - 1 - ctx_place) * local_rows
    visiting = visit_partner(query4[half_rows:])
    second_set = (visiting, partner_start + half_rows + jnp.arange(half_rows, dtype=jnp.int32))
    row_sets = (first_set, second_set)

    def add_tail(tails, key_block, value_block, key_pos):
        pick = (key_pos[None, :] == own_start - WIN + tail_offsets[:, None]).astype(jnp.bfloat16)
        return (
            tails[0]
            + jnp.einsum("wk,kgd->wgd", pick, key_block, preferred_element_type=jnp.float32),
            tails[1]
            + jnp.einsum("wk,kgd->wgd", pick, value_block, preferred_element_type=jnp.float32),
        )

    part_zero = (
        jnp.full((groups, group_ratio, half_rows), big_negative, jnp.float32),
        jnp.zeros((groups, group_ratio, half_rows), jnp.float32),
        jnp.zeros((groups, group_ratio, half_rows, HEAD_SIZE), jnp.float32),
    )
    tail_zero = (
        jnp.zeros((WIN, groups, HEAD_SIZE), jnp.float32),
        jnp.zeros((WIN, groups, HEAD_SIZE), jnp.float32),
    )
    state_zero = (
        jnp.zeros((groups, group_ratio, 2 * FM, HEAD_SIZE), jnp.float32),
        jnp.zeros((groups, group_ratio, 2 * FM), jnp.float32),
    )
    carry = ((part_zero, part_zero), tail_zero, ())
    key_piece = lax.all_gather(keys, "ctx", axis=0, tiled=True)
    value_piece = lax.all_gather(values, "ctx", axis=0, tiled=True)
    piece_rows = key_piece.shape[0]
    stride = math.gcd(piece_rows, local_rows)
    count = piece_rows // stride
    key_blocks = key_piece.reshape(count, stride, groups, HEAD_SIZE)
    value_blocks = value_piece.reshape(count, stride, groups, HEAD_SIZE)

    def fold_step(state, inputs):
        key_block, value_block, number = inputs
        first = number * stride
        key_pos = first + jnp.arange(stride, dtype=jnp.int32)
        parts_now, tails_now, states_now = state
        new_parts = (
            advance(parts_now[0], row_sets[0], key_block, value_block, key_pos, first),
            advance(parts_now[1], row_sets[1], key_block, value_block, key_pos, first),
        )
        earlier_block = first < own_start
        new_tails = lax.cond(
            earlier_block,
            lambda current: add_tail(current, key_block, value_block, key_pos),
            lambda current: current,
            tails_now,
        )
        return ((new_parts, new_tails, states_now), None)

    carry, unused = lax.scan(
        fold_step, carry, (key_blocks, value_blocks, jnp.arange(count, dtype=jnp.int32))
    )
    phi_own = features(proj_own)
    local_kv = split_product("grkf,kgd->grfd", phi_own, own_values)
    state_kv, state_norm = carried_in(
        (local_kv, jnp.sum(phi_own, axis=2)), "ctx", add_pair, state_zero
    )
    parts_done, tails_done = (carry[0], carry[1])
    teacher_first = parts_done[0][2] / parts_done[0][1][..., None]
    teacher_second = parts_done[1][2] / parts_done[1][1][..., None]
    teacher_second = return_partner(teacher_second)
    teacher = jnp.concatenate([teacher_first, teacher_second], axis=2)
    tail_key = tails_done[0].astype(jnp.bfloat16)
    tail_value = tails_done[1].astype(jnp.bfloat16)
    slab_key = jnp.concatenate([tail_key, own_keys], axis=0)
    slab_value = jnp.concatenate([tail_value, own_values], axis=0).astype(jnp.float32)
    slab_rows = WIN + local_rows
    slab_pos = own_start - WIN + jnp.arange(slab_rows, dtype=jnp.int32)
    is_tail = jnp.arange(slab_rows, dtype=jnp.int32) < WIN
    proj_tail = jnp.einsum("kgd,grdf->grkf", tail_key, weight4, preferred_element_type=jnp.float32)
    proj_slab = jnp.concatenate([proj_tail, proj_own], axis=2)
    phi_slab = features(proj_slab)
    proj_query = jnp.einsum("qgrd,grdf->grqf", query4, weight4, preferred_element_type=jnp.float32)
    phi_query = features(proj_query)
    scores = (
        jnp.einsum("qgrd,kgd->grqk", query4, slab_key, preferred_element_type=jnp.float32) * scale
    )
    window = (
        (slab_pos[None, :] >= query_pos[:, None] - WIN)
        & (slab_pos[None, :] <= query_pos[:, None])
        & (slab_pos[None, :] >= 0)
    )
    far = jnp.logical_not(is_tail)[None, :] & (slab_pos[None, :] < query_pos[:, None] - WIN)
    coefficient = far.astype(jnp.float32) - (window & is_tail[None, :]).astype(jnp.float32)
    window_top = jnp.max(jnp.where(window, scores, big_negative), axis=-1)
    local = jnp.exp(jnp.where(window, scores - window_top[..., None], big_negative))
    kernel = jnp.einsum("grqf,grkf->grqk", phi_query, phi_slab, precision=highest)
    mixed = local + coefficient * kernel
    numerator = jnp.einsum("grqk,kgd->grqd", mixed, slab_value, precision=highest) + jnp.einsum(
        "grqf,grfd->grqd", phi_query, state_kv, precision=highest
    )
    denominator = jnp.sum(mixed, axis=-1) + jnp.einsum(
        "grqf,grf->grq", phi_query, state_norm, precision=highest
    )
    student = numerator / denominator[..., None]
    error = student - teacher
    attn_error = jnp.transpose(error, (2, 0, 1, 3)).reshape(local_rows, heads_here * HEAD_SIZE)
    whole_rows = local_rows * ctx_count
    loss = lax.psum(jnp.sum(error * error), ("ctx", "head")) / (whole_rows * QUERY_HEADS)
    grad_out = 2.0 * error / denominator[..., None]
    grad_den = -jnp.sum(grad_out * student, axis=-1)
    later_kv = jnp.einsum("grqf,grqd->grfd", phi_query, grad_out, precision=highest)
    later_norm = jnp.einsum("grqf,grq->grf", phi_query, grad_den, precision=highest)
    suffix_kv, suffix_norm = prefix((later_kv, later_norm), "ctx", add_pair, state_zero)
    grad_lin = coefficient * (
        jnp.einsum("grqd,kgd->grqk", grad_out, slab_value, precision=highest) + grad_den[..., None]
    )
    grad_phi_query = (
        jnp.einsum("grqk,grkf->grqf", grad_lin, phi_slab, precision=highest)
        + jnp.einsum("grqd,grfd->grqf", grad_out, state_kv, precision=highest)
        + grad_den[..., None] * state_norm[:, :, None, :]
    )
    grad_phi_slab = jnp.einsum("grqk,grqf->grkf", grad_lin, phi_query, precision=highest)
    own_extra = (
        jnp.einsum("kgd,grfd->grkf", own_values.astype(jnp.float32), suffix_kv, precision=highest)
        + suffix_norm[:, :, None, :]
    )
    grad_phi_slab = grad_phi_slab + jnp.concatenate(
        [jnp.zeros((groups, group_ratio, WIN, 2 * FM), jnp.float32), own_extra], axis=2
    )
    grad_proj_query = feature_back(proj_query, grad_phi_query)
    grad_proj_slab = feature_back(proj_slab, grad_phi_slab)
    grad_local = jnp.einsum(
        "qgrd,grqf->grdf", query4.astype(jnp.float32), grad_proj_query, precision=highest
    ) + jnp.einsum(
        "kgd,grkf->grdf", slab_key.astype(jnp.float32), grad_proj_slab, precision=highest
    )
    grad_w = lax.psum(grad_local.reshape(heads_here, HEAD_SIZE, FM), "ctx")
    return (attn_error, loss, grad_w)


def solution(mesh):
    placed = (P("ctx", "head"), P("ctx", "head"), P("ctx", "head"), P("head", None, None))
    return jax.shard_map(
        shards,
        mesh=mesh,
        in_specs=placed,
        out_specs=(P("ctx", "head"), P(), P("head", None, None)),
        check_vma=False,
    )
```

profile of v0, /device:TPU:0, one launch (start us, length us, event | category | flops | bytes accessed | tf_op | source)
XLA Modules:
  0.0 783.3 jit_solution(9861084651910707477)
XLA Ops:
  25.6 4.3 fusion.116
  29.9 8.6 %collective-permute-done.1 = bf16[64,4,8,128]{3,2,1,0:T(8,128)(2,1)} collective-permute-done((bf16[64,4,8,128]{3,2,1,0:T(8,128)(2,1)}, bf16[64,4,8,128]{3,2,1,0:T(8,128)(2,1)}, u32[]{:S(2)}, u32[]{:S(2)}) %collective-permute-start.1) | collective-permute-done | bytes 524320 | tf_op jit(solution)/shard_map/ppermute | solution.py:20
  40.3 5.5 fusion.79
  45.8 13.8 %collective-permute-done.2 = bf16[64,4,8,128]{3,2,1,0:T(8,128)(2,1)} collective-permute-done((bf16[64,4,8,128]{3,2,1,0:T(8,128)(2,1)}, bf16[64,4,8,128]{3,2,1,0:T(8,128)(2,1)}, u32[]{:S(2)}, u32[]{:S(2)}) %collective-permute-start.2) | collective-permute-done | bytes 524320 | tf_op jit(solution)/shard_map/ppermute | solution.py:20
  64.5 4.3 maximum_multiply_fusion.1
  68.9 20.4 %collective-permute-done.3 = bf16[64,4,8,128]{3,2,1,0:T(8,128)(2,1)} collective-permute-done((bf16[64,4,8,128]{3,2,1,0:T(8,128)(2,1)}, bf16[64,4,8,128]{3,2,1,0:T(8,128)(2,1)}, u32[]{:S(2)}, u32[]{:S(2)}) %collective-permute-start.3) | collective-permute-done | bytes 524320 | tf_op jit(solution)/shard_map/ppermute | solution.py:20
  91.4 4.4 reshape.276
  95.8 16.4 %all-gather.11.cloned.1.call-done = bf16[2048,512]{1,0:T(8,128)(2,1)} async-done(((bf16[128,512]{1,0:T(8,128)(2,1)}), bf16[2048,512]{1,0:T(8,128)(2,1)}) %all-gather.11.cloned.1.call-update) | async-done | bytes 2097168 | tf_op jit(solution)/shard_map/all_gather | solution.py:198
  112.2 4.0 reshape.277
  118.3 193.6 %while.59 = (s32[]{:T(128)}, f32[4,8,64]{2,1,0:T(8,128)S(1)}, f32[4,8,64]{2,1,0:T(8,128)S(1)}, f32[4,8,64,128]{3,2,1,0:T(8,128)S(1)}, f32[4,8,64]{2,1,0:T(8,128)...) while((s32[]{:T(128)}, f32[4,8,64]{2,1,0:T(8,128)S(1)}, ...), condition=%wide.region_17.18_spmd.clone, body=%wide.region_0.17_spmd.clone.sunk | while | flops 291086528 | bytes 14226523 | solution.py:223
  316.5 64.0 %all-gather.1 = bf16[64,8,128]{2,1,0:T(8,128)(2,1)} all-gather(bf16[4,8,128]{2,1,0:T(8,128)(2,1)S(1)} %fusion.143), channel_id=3, replica_groups=mesh['ctx'=16,'head'=2] {'ctx'}, dimensions={0}, use_global_device_ids=true | all-gather | bytes 139264 | tf_op jit(solution)/shard_map/all_gather | solution.py:26
  384.5 4.6 fusion.46
  389.1 4.7 fusion.109
  393.8 4.8 collective-permute-done.5
  400.9 11.1 %collective-permute-done.6 = bf16[4,8,64,128]{3,2,1,0:T(8,128)(2,1)S(1)} collective-permute-done((bf16[4,8,64,128]{3,2,1,0:T(8,128)(2,1)S(1)}, bf16[4,8,64,128]{3,2,1,0:T(8,128)(2,1)S(1)}, u32[]{:S(2)}, u32[]{:S(2)}) %collective-permute-start.6) | collective-permute-done | bytes 524320 | tf_op jit(solution)/shard_map/ppermute | solution.py:20
  413.3 5.2 fusion.122
  418.5 18.1 %collective-permute-done.7 = bf16[4,8,64,128]{3,2,1,0:T(8,128)(2,1)S(1)} collective-permute-done((bf16[4,8,64,128]{3,2,1,0:T(8,128)(2,1)S(1)}, bf16[4,8,64,128]{3,2,1,0:T(8,128)(2,1)S(1)}, u32[]{:S(2)}, u32[]{:S(2)}) %collective-permute-start.7) | collective-permute-done | bytes 524320 | tf_op jit(solution)/shard_map/ppermute | solution.py:20
  437.7 49.1 %while.60 = (s32[]{:T(128)}, f32[4,8,128,128]{3,2,1,0:T(8,128)S(1)}, f32[4,8,128]{2,1,0:T(8,128)S(1)}, s32[]{:T(128)}, bf16[16,4,8,128,128]{4,3,2,1,0:T(8,128)(2...) while((s32[]{:T(128)}, f32[4,8,128,128]{3,2,1,0:T(8,128)S(1)}, ...), condition=%wide.region_21.22_spmd.clone, body=%wide.region_20.21_spmd.clone.sunk | while | flops 2113540 | bytes 5283955 | solution.py:43
  486.7 5.7 fusion.150
  492.5 6.4 multiply_reduce_fusion
  500.2 4.6 convolution_convert_fusion
  505.4 3.6 fusion.151
  509.0 19.1 %all-gather.3 = bf16[64,8,128]{2,1,0:T(8,128)(2,1)S(1)} all-gather(bf16[4,8,128]{2,1,0:T(8,128)(2,1)S(1)} %convert_element_type.142), channel_id=5, replica_groups=mesh['ctx'=16,'head'=2] {'ctx'}, dimensions={0}, use_global_device_ids=true | all-gather | bytes 139264 | tf_op jit(solution)/shard_map/all_gather | solution.py:49
  531.3 7.9 %fusion.68 = f32[4,8,128,128]{3,2,1,0:T(8,128)S(1)} fusion(f32[4,8,128,192]{2,3,1,0:T(8,128)S(1)} %fusion.121, f32[4,8,128]{2,1,0:T(8,128)S(1)} %neg.21, f32[128,192]{0,1:T(8,128)S(1)} %convert_subtract_fusion, f32[4,8,192,64]{3,2,1,0:T(8,128)S(1)} %copy-done.11, f32[4,8,192,64]{3,2,1,0:T(8,128)S(1)} %copy-done.9), kind=kOutput, calls=%fused_computation.116 | convolution fusion | flops 1211105280 | bytes 8503296 | tf_op jit(solution)/shard_map/grqk,grkf->grqf/dot_general | solution.py:282
  539.2 4.8 multiply_add_fusion.4
  544.1 4.5 fusion.83
  548.6 81.4 %all-gather.15.cloned.1.call-done = bf16[64,8,128,128]{3,2,1,0:T(8,128)(2,1)} async-done(((bf16[4,8,128,128]{3,2,1,0:T(8,128)(2,1)}), bf16[64,8,128,128]{3,2,1,0:T(8,128)(2,1)}) %all-gather.15.cloned.1.call-update) | async-done | bytes 16777232 | tf_op jit(solution)/shard_map/all_gather | solution.py:49
  630.0 38.6 %while.61 = (s32[]{:T(128)}, f32[4,8,128,128]{3,2,1,0:T(8,128)S(1)}, f32[4,8,128]{2,1,0:T(8,128)S(1)}, s32[]{:T(128)}, bf16[16,4,8,128,128]{4,3,2,1,0:T(8,128)(2...) while((s32[]{:T(128)}, ...), condition=%wide.region_27.28_spmd.clone, body=%wide.region_26.27_spmd.clone.sunk | while | flops 2113544 | bytes 5284017 | solution.py:67
  670.2 5.7 pad_add_fusion
  675.9 5.3 fusion.102
  681.2 39.0 %psum.14 = f32[]{:T(128)} all-reduce(f32[]{:T(128)} %get-tuple-element.673), channel_id=1, replica_groups=mesh['ctx'=16,'head'=2] {'ctx','head'}, use_global_device_ids=true, to_apply=%region_24.25 | all-reduce | flops 1 | bytes 8 | tf_op jit(solution)/shard_map/psum | solution.py:272
  724.6 48.3 %all-reduce.3.cloned.1.call-done = f32[32,128,64]{1,2,0:T(8,128)} async-done(((f32[32,128,64]{1,2,0:T(8,128)}), f32[32,128,64]{1,2,0:T(8,128)}) %all-reduce.3.cloned.1.call-update) | async-done | bytes 1048592 | tf_op jit(solution)/shard_map/psum | solution.py:301
  (483 shorter events, 321.2 us)
Async XLA Ops:
  7.2 84.2 %all-gather.9.cloned.1.call-start = ((), (), s32[]{:S(2)}) async-start(), calls=%async_computation | async-start | bytes 2228224 | tf_op jit(solution)/shard_map/all_gather | solution.py:197
  7.9 104.2 %all-gather.11.cloned.1.call-start = ((), (), s32[]{:S(2)}) async-start(), calls=%async_computation.1 | async-start | bytes 2228224 | tf_op jit(solution)/shard_map/all_gather | solution.py:198
  8.7 429.0 %all-gather.13.cloned.1.call-start = ((), (), s32[]{:S(2)}) async-start(), calls=%async_computation.3 | async-start | bytes 17825792 | tf_op jit(solution)/shard_map/all_gather | solution.py:26
  10.8 53.0 %copy-start.22 = (bf16[128,512]{0,1:T(8,128)(2,1)}, bf16[128,512]{0,1:T(8,128)(2,1)S(1)}, u32[]{:S(2)}) copy-start(bf16[128,512]{0,1:T(8,128)(2,1)S(1)} %copy.138) | copy-start | bytes 393220
  17.9 612.1 %all-gather.15.cloned.1.call-start = ((), (), s32[]{:S(2)}) async-start(), calls=%async_computation.4 | async-start | bytes 17825792 | tf_op jit(solution)/shard_map/all_gather | solution.py:49
  20.1 2.9 collective-permute-start
  23.1 15.4 %collective-permute-start.1 = (bf16[64,4,8,128]{3,2,1,0:T(8,128)(2,1)}, bf16[64,4,8,128]{3,2,1,0:T(8,128)(2,1)}, u32[]{:S(2)}, u32[]{:S(2)}) collective-permute-start(bf16[64,4,8,128]{3,2,1,0:T(8,128)(2,1)} %collective-permute-done), channel_id=1, source_target_pairs={{0,4},{2,6},{4,0},{6,2},{8,12},{10,14},{12,8},{14,10},{16,20},{18,... | collective-permute-start | bytes 1572872 | tf_op jit(solution)/shard_map/ppermute | solution.py:20
  29.9 16.0 %copy-start.28 = (u8[4,128,64]{2,1,0:T(8,128)(4,1)}, u8[4,128,64]{2,1,0:T(8,128)(4,1)S(1)}, u32[]{:S(2)}) copy-start(u8[4,128,64]{2,1,0:T(8,128)(4,1)S(1)} %get-tuple-element.671) | copy-start | bytes 98308
  38.5 21.1 %collective-permute-start.2 = (bf16[64,4,8,128]{3,2,1,0:T(8,128)(2,1)}, bf16[64,4,8,128]{3,2,1,0:T(8,128)(2,1)}, u32[]{:S(2)}, u32[]{:S(2)}) collective-permute-start(bf16[64,4,8,128]{3,2,1,0:T(8,128)(2,1)} %collective-permute-done.1), channel_id=1, source_target_pairs={{0,8},{2,10},{4,12},{6,14},{8,0},{10,2},{12,4},{14,6},{16,24},{18,... | collective-permute-start | bytes 1572872 | tf_op jit(solution)/shard_map/ppermute | solution.py:20
  40.3 21.7 %copy-start.14 = (f32[4,8,128,64]{3,2,1,0:T(8,128)S(1)}, f32[4,8,128,64]{3,2,1,0:T(8,128)}, u32[]{:S(2)}) copy-start(f32[4,8,128,64]{3,2,1,0:T(8,128)} %copy-done.13) | copy-start | bytes 3145732
  59.6 29.8 %collective-permute-start.3 = (bf16[64,4,8,128]{3,2,1,0:T(8,128)(2,1)}, bf16[64,4,8,128]{3,2,1,0:T(8,128)(2,1)}, u32[]{:S(2)}, u32[]{:S(2)}) collective-permute-start(bf16[64,4,8,128]{3,2,1,0:T(8,128)(2,1)} %collective-permute-done.2), channel_id=1, source_target_pairs={{0,16},{2,18},{4,20},{6,22},{8,24},{10,26},{12,28},{14,30},{16,0},... | collective-permute-start | bytes 1572872 | tf_op jit(solution)/shard_map/ppermute | solution.py:20
  313.0 71.4 %collective-permute-start.4 = (bf16[4,8,64,128]{3,2,1,0:T(8,128)(2,1)}, bf16[4,8,64,128]{3,2,1,0:T(8,128)(2,1)S(1)}, u32[]{:S(2)}, u32[]{:S(2)}) collective-permute-start(bf16[4,8,64,128]{3,2,1,0:T(8,128)(2,1)} %divide_convert_fusion), channel_id=1, source_target_pairs={{0,2},{2,0},{4,6},{6,4},{8,10},{10,8},{12,14},{14,12},{16,18},{18,... | collective-permute-start | bytes 1572872 | tf_op jit(solution)/shard_map/ppermute | solution.py:20
  384.4 14.2 %collective-permute-start.5 = (bf16[4,8,64,128]{3,2,1,0:T(8,128)(2,1)S(1)}, bf16[4,8,64,128]{3,2,1,0:T(8,128)(2,1)S(1)}, u32[]{:S(2)}, u32[]{:S(2)}) collective-permute-start(bf16[4,8,64,128]{3,2,1,0:T(8,128)(2,1)S(1)} %collective-permute-done.4), channel_id=1, source_target_pairs={{0,4},{2,6},{4,0},{6,2},{8,12},{10,14},{12,8},{14,10},{16,20},{18,... | collective-permute-start | bytes 1572872 | tf_op jit(solution)/shard_map/ppermute | solution.py:20
  389.1 9.6 %copy-start.20 = (bf16[16,8,32,128]{3,2,1,0:T(8,128)(2,1)S(1)}, bf16[16,8,32,128]{3,2,1,0:T(8,128)(2,1)}, u32[]{:S(2)}) copy-start(bf16[16,8,32,128]{3,2,1,0:T(8,128)(2,1)} %copy.204) | copy-start | bytes 3145732
  389.1 9.6 %copy-start.27 = (bf16[128,4,128]{2,0,1:T(8,128)(2,1)S(1)}, bf16[128,4,128]{2,0,1:T(8,128)(2,1)}, u32[]{:S(2)}) copy-start(bf16[128,4,128]{2,0,1:T(8,128)(2,1)} %copy.128) | copy-start | bytes 393220
  393.8 5.5 copy-start.17
  398.6 13.4 %collective-permute-start.6 = (bf16[4,8,64,128]{3,2,1,0:T(8,128)(2,1)S(1)}, bf16[4,8,64,128]{3,2,1,0:T(8,128)(2,1)S(1)}, u32[]{:S(2)}, u32[]{:S(2)}) collective-permute-start(bf16[4,8,64,128]{3,2,1,0:T(8,128)(2,1)S(1)} %collective-permute-done.5), channel_id=1, source_target_pairs={{0,8},{2,10},{4,12},{6,14},{8,0},{10,2},{12,4},{14,6},{16,24},{18,... | collective-permute-start | bytes 1572872 | tf_op jit(solution)/shard_map/ppermute | solution.py:20
  400.9 12.4 %copy-start.26 = (bf16[128,4,128]{2,0,1:T(8,128)(2,1)S(1)}, bf16[128,4,128]{2,0,1:T(8,128)(2,1)}, u32[]{:S(2)}) copy-start(bf16[128,4,128]{2,0,1:T(8,128)(2,1)} %copy.139) | copy-start | bytes 393220
  412.0 24.6 %collective-permute-start.7 = (bf16[4,8,64,128]{3,2,1,0:T(8,128)(2,1)S(1)}, bf16[4,8,64,128]{3,2,1,0:T(8,128)(2,1)S(1)}, u32[]{:S(2)}, u32[]{:S(2)}) collective-permute-start(bf16[4,8,64,128]{3,2,1,0:T(8,128)(2,1)S(1)} %collective-permute-done.6), channel_id=1, source_target_pairs={{0,16},{2,18},{4,20},{6,22},{8,24},{10,26},{12,28},{14,30},{16,0},... | collective-permute-start | bytes 1572872 | tf_op jit(solution)/shard_map/ppermute | solution.py:20
  413.3 24.3 %copy-start.2 = (f32[4,8,128,128]{3,2,1,0:T(8,128)S(1)}, f32[4,8,128,128]{3,2,1,0:T(8,128)}, u32[]{:S(2)}) copy-start(f32[4,8,128,128]{3,2,1,0:T(8,128)} %custom-call) | copy-start | bytes 6291460
  486.7 12.1 %copy-start.3 = (f32[4,8,128,128]{3,2,1,0:T(8,128)}, f32[4,8,128,128]{3,2,1,0:T(8,128)S(1)}, u32[]{:S(2)}) copy-start(f32[4,8,128,128]{3,2,1,0:T(8,128)S(1)} %get-tuple-element.496) | copy-start | bytes 6291460
  486.7 5.8 copy-start.6
  504.8 268.1 %all-reduce.3.cloned.1.call-start = ((), (), s32[]{:S(2)}) async-start(), calls=%async_computation.2 | async-start | bytes 2097152 | tf_op jit(solution)/shard_map/psum | solution.py:301
  505.3 25.9 %copy-start.11 = (f32[4,8,192,64]{3,2,1,0:T(8,128)S(1)}, f32[4,8,192,64]{3,2,1,0:T(8,128)}, u32[]{:S(2)}) copy-start(f32[4,8,192,64]{3,2,1,0:T(8,128)} %copy-done.10) | copy-start | bytes 4718596
  531.3 7.9 %copy-start.12 = (f32[4,8,128,192]{2,3,1,0:T(8,128)}, f32[4,8,128,192]{2,3,1,0:T(8,128)S(1)}, u32[]{:S(2)}) copy-start(f32[4,8,128,192]{2,3,1,0:T(8,128)S(1)} %fusion.121) | copy-start | bytes 9437188
  531.3 7.9 %copy-start.4 = (f32[4,8,128,128]{3,2,1,0:T(8,128)S(1)}, f32[4,8,128,128]{3,2,1,0:T(8,128)}, u32[]{:S(2)}) copy-start(f32[4,8,128,128]{3,2,1,0:T(8,128)} %copy-done.3) | copy-start | bytes 6291460
  531.3 7.9 %copy-start.16 = (f32[4,8,128,128]{3,2,1,0:T(8,128)S(1)}, f32[4,8,128,128]{3,2,1,0:T(8,128)}, u32[]{:S(2)}) copy-start(f32[4,8,128,128]{3,2,1,0:T(8,128)} %copy-done.15) | copy-start | bytes 6291460
  630.0 38.6 %copy-start.23 = (bf16[128,512]{0,1:T(8,128)(2,1)S(1)}, bf16[128,512]{0,1:T(8,128)(2,1)}, u32[]{:S(2)}) copy-start(bf16[128,512]{0,1:T(8,128)(2,1)} %copy-done.22) | copy-start | bytes 393220
  670.2 5.7 copy-start.19
  670.2 5.8 copy-start.25
  670.2 5.8 copy-start.31
  722.1 53.1 %copy-start.1 = (bf16[32,128,64]{1,2,0:T(8,128)(2,1)S(1)}, bf16[32,128,64]{1,2,0:T(8,128)(2,1)}, u32[]{:S(2)}) copy-start(bf16[32,128,64]{1,2,0:T(8,128)(2,1)} %param.21) | copy-start | bytes 1572868
  (13 other events, 49.1 us)
Sparse Core Ops, SparseCore 0:
  10.2 45.6 all-gather.8
  58.0 54.1 all-gather.10
  114.3 125.7 all-gather.12
  505.0 124.9 all-gather.14
  681.3 91.5 all-reduce.2
where the time goes:
time: 796 us; the launch traced here: 783 us
  waiting for transfers between devices  224 us (28%)
  blocking collectives  122 us (15%)
  matrix products  120 us (15%)
  other arithmetic  120 us (15%)
  local copies, waits for them, and re-layouts  96.2 us (12%)
  loops' own time  72.7 us (9%)
  between operations  16.5 us (2%)
  starting transfers between devices  11 us (1%)
    all_gather x1, waiting for transfers between devices, prefix(): lax.all_gather(part.astype(kind), axis)  81.4 us
    ppermute x8, waiting for transfers between devices, swapped(): return lax.ppermute(value, axis, pairs)  76.8 us
    another operation x1, loops' own time, shards(): lax.scan(fold_step, carry, (key_blocks, value_blocks, jnp.arange(count, d...  70.5 us
    all_gather x1, blocking collectives, carried_in(): lax.all_gather(part.astype(kind), axis)  64 us
    select_n x32, other arithmetic, carried_step(): return jax.tree.map(lambda a, b: jnp.where(reached, a, b), new, before)  49 us
    psum x1, waiting for transfers between devices, shards(): grad_w = lax.psum(grad_local.reshape(heads_here, HEAD_SIZE, FM), 'ctx')  48.3 us
    psum x1, blocking collectives, shards(): lax.psum(jnp.sum(error * error), ('ctx', 'head'))  39 us
    dynamic_slice x64, local copies, waits for them, and re-layouts, shards(): lax.scan(fold_step, carry, (key_blocks, value_blocks, jnp.arange(count, d...  38.7 us
  transfers between devices with their start and end apart: 13, of which 9 were waited for; matrix products, arithmetic and copies ran while one was open for 28% of the time, Pallas kernels for 0%

commit v1 on v0

--- a/solution.py
+++ b/solution.py
@@ -12,6 +12,22 @@
 phi_scale = 0.00390625
 big_negative = -1e30
 highest = lax.Precision.HIGHEST
+
+
+def gather_around(x, axis, dim):
+    ways, here, step = (lax.axis_size(axis), lax.axis_index(axis), x.shape[dim])
+    shape = [n * ways if d == dim else n for d, n in enumerate(x.shape)]
+    full = lax.dynamic_update_slice_in_dim(jnp.zeros(shape, x.dtype), x, here * step, axis=dim)
+    going_up = going_down = x
+    for far in range(1, ways // 2 + 1):
+        going_up = lax.ppermute(going_up, axis, [(d, (d + 1) % ways) for d in range(ways)])
+        full = lax.dynamic_update_slice_in_dim(full, going_up, (here - far) % ways * step, axis=dim)
+        if 2 * far < ways:
+            going_down = lax.ppermute(going_down, axis, [(d, (d - 1) % ways) for d in range(ways)])
+            full = lax.dynamic_update_slice_in_dim(
+                full, going_down, (here + far) % ways * step, axis=dim
+            )
+    return full
 
 
 def swapped(value, axis, distance):
@@ -195,7 +211,7 @@
     )
     carry = ((part_zero, part_zero), tail_zero, ())
     key_piece = lax.all_gather(keys, "ctx", axis=0, tiled=True)
-    value_piece = lax.all_gather(values, "ctx", axis=0, tiled=True)
+    value_piece = gather_around(values, "ctx", 0)
     piece_rows = key_piece.shape[0]
     stride = math.gcd(piece_rows, local_rows)
     count = piece_rows // stride

time: 796 us -> 832 us (1.045)
  starting transfers between devices: 11 us -> 48 us
  local copies, waits for them, and re-layouts: 96.2 us -> 108 us
  waiting for transfers between devices: 224 us -> 213 us
  blocking collectives: 122 us -> 131 us
    ppermute x0 -> x15, waiting for transfers between devices: none -> 50.9 us  [the longest x8 38.1 us: gather_around(): lax.ppermute(going_up, axis, [(d, (d + 1) % ways) for d in range(ways)])]
    ppermute x8, waiting for transfers between devices: 76.8 us -> 32.8 us  [swapped(): return lax.ppermute(value, axis, pairs)]
    ppermute x0 -> x15, starting transfers between devices: none -> 38.2 us  [the longest x7 30.4 us: gather_around(): lax.ppermute(going_down, axis, [(d, (d - 1) % ways) for d in range(ways)])]
    all_gather x1 -> x0, waiting for transfers between devices: 16.4 us -> none  [shards(): value_piece = lax.all_gather(values, 'ctx', axis=0, tiled=True)]
    squeeze x0 -> x16, local copies, waits for them, and re-layouts: none -> 15.2 us  [shards(): lax.scan(fold_step, carry, (key_blocks, value_blocks, jnp.arange(count, d...]
    dynamic_slice x64 -> x32, local copies, waits for them, and re-layouts: 38.7 us -> 24.9 us  [shards(): lax.scan(fold_step, carry, (key_blocks, value_blocks, jnp.arange(count, d...]
    ppermute x0 -> x15, local copies, waits for them, and re-layouts: none -> 11.8 us  [the longest x8 6.42 us: gather_around(): lax.ppermute(going_up, axis, [(d, (d + 1) % ways) for d in range(ways)])]
    unnamed x74 -> x88, local copies, waits for them, and re-layouts: 14.9 us -> 24.7 us
  transfers between devices with their start and end apart: 13 -> 27, of which waited for: 9 -> 17; matrix products, arithmetic and copies ran while one was open for 28% -> 27% of each run, Pallas kernels for 0% -> 0%
where the time goes in v1:
time: 832 us; the launch traced here: 818 us
  waiting for transfers between devices  213 us (26%)
  blocking collectives  131 us (16%)
  matrix products  118 us (14%)
  other arithmetic  114 us (14%)
  local copies, waits for them, and re-layouts  108 us (13%)
  loops' own time  70 us (8%)
  starting transfers between devices  48 us (6%)
  between operations  17.1 us (2%)
    all_gather x1, waiting for transfers between devices, prefix(): lax.all_gather(part.astype(kind), axis)  80.1 us
    all_gather x1, blocking collectives, carried_in(): lax.all_gather(part.astype(kind), axis)  72 us
    another operation x1, loops' own time, shards(): lax.scan(fold_step, carry, (key_blocks, value_blocks, jnp.arange(count, d...  67.6 us
    select_n x32, other arithmetic, carried_step(): return jax.tree.map(lambda a, b: jnp.where(reached, a, b), new, before)  49 us
    psum x1, waiting for transfers between devices, shards(): grad_w = lax.psum(grad_local.reshape(heads_here, HEAD_SIZE, FM), 'ctx')  48.3 us
    psum x1, blocking collectives, shards(): lax.psum(jnp.sum(error * error), ('ctx', 'head'))  38.9 us
    ppermute x8, waiting for transfers between devices, gather_around(): lax.ppermute(going_up, axis, [(d, (d + 1) % ways) for d in range(ways)])  38.1 us
    select_n x32, other arithmetic, prefix_step(): return jax.tree.map(lambda a, b: jnp.where(reached, a, b), new, before)  38 us
  transfers between devices with their start and end apart: 27, of which 17 were waited for; matrix products, arithmetic and copies ran while one was open for 27% of the time, Pallas kernels for 0%

profile of v1, /device:TPU:0, one launch (start us, length us, event | category | flops | bytes accessed | tf_op | source)
XLA Modules:
  0.0 818.4 jit_solution(3640379099639403416)
XLA Ops:
  17.7 5.1 collective-permute-start.1
  52.0 4.5 collective-permute-start.5
  60.0 4.2 collective-permute-start.6
  75.1 4.7 collective-permute-start.9
  79.9 17.1 %collective-permute-done.8 = bf16[128,512]{1,0:T(8,128)(2,1)} collective-permute-done((bf16[128,512]{1,0:T(8,128)(2,1)}, bf16[128,512]{1,0:T(8,128)(2,1)}, u32[]{:S(2)}, u32[]{:S(2)}) %collective-permute-start.8) | collective-permute-done | bytes 131104 | tf_op jit(solution)/shard_map/ppermute | solution.py:23
  100.2 4.6 collective-permute-start.11
  111.1 4.8 collective-permute-start.13
  122.1 7.9 collective-permute-done.13
  130.1 5.6 collective-permute-done.14
  138.8 4.3 copy.184
  150.6 184.9 %while.59 = (s32[]{:T(128)}, f32[4,8,64]{2,1,0:T(8,128)S(1)}, f32[4,8,64]{2,1,0:T(8,128)S(1)}, f32[4,8,64,128]{3,2,1,0:T(8,128)S(1)}, f32[4,8,64]{2,1,0:T(8,128)...) while((s32[]{:T(128)}, f32[4,8,64]{2,1,0:T(8,128)S(1)}, ...), condition=%wide.region_17.18_spmd.clone, body=%wide.region_0.17_spmd.clone.sunk | while | flops 291086528 | bytes 13964383 | solution.py:239
  335.9 8.0 collective-permute-start.19
  343.9 72.0 %all-gather.1 = bf16[64,8,128]{2,1,0:T(8,128)(2,1)} all-gather(bf16[4,8,128]{2,1,0:T(8,128)(2,1)S(1)} %fusion.143), channel_id=3, replica_groups=mesh['ctx'=16,'head'=2] {'ctx'}, dimensions={0}, use_global_device_ids=true | all-gather | bytes 139264 | tf_op jit(solution)/shard_map/all_gather | solution.py:42
  421.5 4.4 fusion.46
  425.9 4.7 fusion.109
  436.6 11.0 %collective-permute-done.21 = bf16[4,8,64,128]{3,2,1,0:T(8,128)(2,1)S(1)} collective-permute-done((bf16[4,8,64,128]{3,2,1,0:T(8,128)(2,1)S(1)}, bf16[4,8,64,128]{3,2,1,0:T(8,128)(2,1)S(1)}, u32[]{:S(2)}, u32[]{:S(2)}) %collective-permute-start.21) | collective-permute-done | bytes 524320 | tf_op jit(solution)/shard_map/ppermute | solution.py:36
  449.0 5.2 fusion.122
  454.2 18.1 %collective-permute-done.22 = bf16[4,8,64,128]{3,2,1,0:T(8,128)(2,1)S(1)} collective-permute-done((bf16[4,8,64,128]{3,2,1,0:T(8,128)(2,1)S(1)}, bf16[4,8,64,128]{3,2,1,0:T(8,128)(2,1)S(1)}, u32[]{:S(2)}, u32[]{:S(2)}) %collective-permute-start.22) | collective-permute-done | bytes 524320 | tf_op jit(solution)/shard_map/ppermute | solution.py:36
  473.3 49.1 %while.60 = (s32[]{:T(128)}, f32[4,8,128,128]{3,2,1,0:T(8,128)S(1)}, f32[4,8,128]{2,1,0:T(8,128)S(1)}, s32[]{:T(128)}, bf16[16,4,8,128,128]{4,3,2,1,0:T(8,128)(2...) while((s32[]{:T(128)}, f32[4,8,128,128]{3,2,1,0:T(8,128)S(1)}, ...), condition=%wide.region_21.22_spmd.clone, body=%wide.region_20.21_spmd.clone.sunk | while | flops 2113540 | bytes 5283955 | solution.py:59
  522.4 5.7 fusion.150
  528.2 6.4 multiply_reduce_fusion
  535.8 4.6 convolution_convert_fusion
  544.6 20.0 %all-gather.3 = bf16[64,8,128]{2,1,0:T(8,128)(2,1)S(1)} all-gather(bf16[4,8,128]{2,1,0:T(8,128)(2,1)S(1)} %convert_element_type.142), channel_id=5, replica_groups=mesh['ctx'=16,'head'=2] {'ctx'}, dimensions={0}, use_global_device_ids=true | all-gather | bytes 139264 | tf_op jit(solution)/shard_map/all_gather | solution.py:65
  567.9 7.9 fusion.68
  575.8 4.8 multiply_add_fusion.4
  580.6 4.5 fusion.83
  585.2 80.1 %all-gather.12.cloned.1.call-done = bf16[64,8,128,128]{3,2,1,0:T(8,128)(2,1)} async-done(((bf16[4,8,128,128]{3,2,1,0:T(8,128)(2,1)}), bf16[64,8,128,128]{3,2,1,0:T(8,128)(2,1)}) %all-gather.12.cloned.1.call-update) | async-done | bytes 16777232 | tf_op jit(solution)/shard_map/all_gather | solution.py:65
  665.2 38.6 %while.61 = (s32[]{:T(128)}, f32[4,8,128,128]{3,2,1,0:T(8,128)S(1)}, f32[4,8,128]{2,1,0:T(8,128)S(1)}, s32[]{:T(128)}, bf16[16,4,8,128,128]{4,3,2,1,0:T(8,128)(2...) while((s32[]{:T(128)}, ...), condition=%wide.region_27.28_spmd.clone, body=%wide.region_26.27_spmd.clone.sunk | while | flops 2113544 | bytes 5284017 | solution.py:83
  705.4 5.7 pad_add_fusion
  711.2 5.3 fusion.102
  716.5 38.9 %psum.14 = f32[]{:T(128)} all-reduce(f32[]{:T(128)} %get-tuple-element.673), channel_id=1, replica_groups=mesh['ctx'=16,'head'=2] {'ctx','head'}, use_global_device_ids=true, to_apply=%region_24.25 | all-reduce | flops 1 | bytes 8 | tf_op jit(solution)/shard_map/psum | solution.py:288
  759.8 48.3 %all-reduce.3.cloned.1.call-done = f32[32,128,64]{1,2,0:T(8,128)} async-done(((f32[32,128,64]{1,2,0:T(8,128)}), f32[32,128,64]{1,2,0:T(8,128)}) %all-reduce.3.cloned.1.call-update) | async-done | bytes 1048592 | tf_op jit(solution)/shard_map/psum | solution.py:317
  (539 shorter events, 370.7 us)
Async XLA Ops:
  7.2 137.9 %all-gather.8.cloned.1.call-start = ((), (), s32[]{:S(2)}) async-start(), calls=%async_computation | async-start | bytes 2228224 | tf_op jit(solution)/shard_map/all_gather | solution.py:213
  7.9 465.4 %all-gather.10.cloned.1.call-start = ((), (), s32[]{:S(2)}) async-start(), calls=%async_computation.2 | async-start | bytes 17825792 | tf_op jit(solution)/shard_map/all_gather | solution.py:42
  10.0 29.1 %copy-start.20 = (bf16[128,512]{0,1:T(8,128)(2,1)}, bf16[128,512]{0,1:T(8,128)(2,1)S(1)}, u32[]{:S(2)}) copy-start(bf16[128,512]{0,1:T(8,128)(2,1)S(1)} %copy.167) | copy-start | bytes 393220
  17.1 648.1 %all-gather.12.cloned.1.call-start = ((), (), s32[]{:S(2)}) async-start(), calls=%async_computation.3 | async-start | bytes 17825792 | tf_op jit(solution)/shard_map/all_gather | solution.py:65
  17.2 22.7 %collective-permute-start = (bf16[128,512]{1,0:T(8,128)(2,1)}, bf16[128,512]{1,0:T(8,128)(2,1)}, u32[]{:S(2)}, u32[]{:S(2)}) collective-permute-start(bf16[128,512]{1,0:T(8,128)(2,1)} %param.20), channel_id=1, source_target_pairs={{0,2},{2,4},{4,6},{6,8},{8,10},{10,12},{12,14},{14,16},{16,18},{18... | collective-permute-start | bytes 393224 | tf_op jit(solution)/shard_map/ppermute | solution.py:23
  17.7 23.8 %collective-permute-start.1 = (bf16[128,512]{1,0:T(8,128)(2,1)}, bf16[128,512]{1,0:T(8,128)(2,1)}, u32[]{:S(2)}, u32[]{:S(2)}) collective-permute-start(bf16[128,512]{1,0:T(8,128)(2,1)} %param.20), channel_id=1, source_target_pairs={{0,30},{2,0},{4,2},{6,4},{8,6},{10,8},{12,10},{14,12},{16,14},{18,... | collective-permute-start | bytes 393224 | tf_op jit(solution)/shard_map/ppermute | solution.py:26
  25.7 15.7 %collective-permute-start.15 = (bf16[64,4,8,128]{3,2,1,0:T(8,128)(2,1)}, bf16[64,4,8,128]{3,2,1,0:T(8,128)(2,1)}, u32[]{:S(2)}, u32[]{:S(2)}) collective-permute-start(bf16[64,4,8,128]{3,2,1,0:T(8,128)(2,1)} %bitcast.101), channel_id=1, source_target_pairs={{0,2},{2,0},{4,6},{6,4},{8,10},{10,8},{12,14},{14,12},{16,18},{18,... | collective-permute-start | bytes 1572872 | tf_op jit(solution)/shard_map/ppermute | solution.py:36
  40.9 9.2 %collective-permute-start.2 = (bf16[128,512]{1,0:T(8,128)(2,1)}, bf16[128,512]{1,0:T(8,128)(2,1)S(1)}, u32[]{:S(2)}, u32[]{:S(2)}) collective-permute-start(bf16[128,512]{1,0:T(8,128)(2,1)} %collective-permute-done), channel_id=1, source_target_pairs={{0,2},{2,4},{4,6},{6,8},{8,10},{10,12},{12,14},{14,16},{16,18},{18... | collective-permute-start | bytes 393224 | tf_op jit(solution)/shard_map/ppermute | solution.py:23
  41.5 27.0 %collective-permute-start.16 = (bf16[64,4,8,128]{3,2,1,0:T(8,128)(2,1)}, bf16[64,4,8,128]{3,2,1,0:T(8,128)(2,1)}, u32[]{:S(2)}, u32[]{:S(2)}) collective-permute-start(bf16[64,4,8,128]{3,2,1,0:T(8,128)(2,1)} %collective-permute-done.15), channel_id=1, source_target_pairs={{0,4},{2,6},{4,0},{6,2},{8,12},{10,14},{12,8},{14,10},{16,20},{18,... | collective-permute-start | bytes 1572872 | tf_op jit(solution)/shard_map/ppermute | solution.py:36
  42.6 8.4 %collective-permute-start.3 = (bf16[128,512]{1,0:T(8,128)(2,1)}, bf16[128,512]{1,0:T(8,128)(2,1)}, u32[]{:S(2)}, u32[]{:S(2)}) collective-permute-start(bf16[128,512]{1,0:T(8,128)(2,1)} %collective-permute-done.1), channel_id=1, source_target_pairs={{0,30},{2,0},{4,2},{6,4},{8,6},{10,8},{12,10},{14,12},{16,14},{18,... | collective-permute-start | bytes 393224 | tf_op jit(solution)/shard_map/ppermute | solution.py:26
  50.8 9.0 %collective-permute-start.4 = (bf16[128,512]{1,0:T(8,128)(2,1)}, bf16[128,512]{1,0:T(8,128)(2,1)S(1)}, u32[]{:S(2)}, u32[]{:S(2)}) collective-permute-start(bf16[128,512]{1,0:T(8,128)(2,1)} %copy-done.32), channel_id=1, source_target_pairs={{0,2},{2,4},{4,6},{6,8},{8,10},{10,12},{12,14},{14,16},{16,18},{18... | collective-permute-start | bytes 393224 | tf_op jit(solution)/shard_map/ppermute | solution.py:23
  52.0 12.6 %collective-permute-start.5 = (bf16[128,512]{1,0:T(8,128)(2,1)}, bf16[128,512]{1,0:T(8,128)(2,1)}, u32[]{:S(2)}, u32[]{:S(2)}) collective-permute-start(bf16[128,512]{1,0:T(8,128)(2,1)} %collective-permute-done.3), channel_id=1, source_target_pairs={{0,30},{2,0},{4,2},{6,4},{8,6},{10,8},{12,10},{14,12},{16,14},{18,... | collective-permute-start | bytes 393224 | tf_op jit(solution)/shard_map/ppermute | solution.py:26
  60.0 9.6 %collective-permute-start.6 = (bf16[128,512]{1,0:T(8,128)(2,1)S(1)}, bf16[128,512]{1,0:T(8,128)(2,1)}, u32[]{:S(2)}, u32[]{:S(2)}) collective-permute-start(bf16[128,512]{1,0:T(8,128)(2,1)S(1)} %collective-permute-done.4), channel_id=1, source_target_pairs={{0,2},{2,4},{4,6},{6,8},{8,10},{10,12},{12,14},{14,16},{16,18},{18... | collective-permute-start | bytes 393224 | tf_op jit(solution)/shard_map/ppermute | solution.py:23
  65.6 8.5 %collective-permute-start.7 = (bf16[128,512]{1,0:T(8,128)(2,1)}, bf16[128,512]{1,0:T(8,128)(2,1)}, u32[]{:S(2)}, u32[]{:S(2)}) collective-permute-start(bf16[128,512]{1,0:T(8,128)(2,1)} %collective-permute-done.5), channel_id=1, source_target_pairs={{0,30},{2,0},{4,2},{6,4},{8,6},{10,8},{12,10},{14,12},{16,14},{18,... | collective-permute-start | bytes 393224 | tf_op jit(solution)/shard_map/ppermute | solution.py:26
  68.4 40.9 %collective-permute-start.17 = (bf16[64,4,8,128]{3,2,1,0:T(8,128)(2,1)}, bf16[64,4,8,128]{3,2,1,0:T(8,128)(2,1)}, u32[]{:S(2)}, u32[]{:S(2)}) collective-permute-start(bf16[64,4,8,128]{3,2,1,0:T(8,128)(2,1)} %collective-permute-done.16), channel_id=1, source_target_pairs={{0,8},{2,10},{4,12},{6,14},{8,0},{10,2},{12,4},{14,6},{16,24},{18,... | collective-permute-start | bytes 1572872 | tf_op jit(solution)/shard_map/ppermute | solution.py:36
  70.6 26.3 %collective-permute-start.8 = (bf16[128,512]{1,0:T(8,128)(2,1)}, bf16[128,512]{1,0:T(8,128)(2,1)}, u32[]{:S(2)}, u32[]{:S(2)}) collective-permute-start(bf16[128,512]{1,0:T(8,128)(2,1)} %collective-permute-done.6), channel_id=1, source_target_pairs={{0,2},{2,4},{4,6},{6,8},{8,10},{10,12},{12,14},{14,16},{16,18},{18... | collective-permute-start | bytes 393224 | tf_op jit(solution)/shard_map/ppermute | solution.py:23
  75.1 24.9 %collective-permute-start.9 = (bf16[128,512]{1,0:T(8,128)(2,1)}, bf16[128,512]{1,0:T(8,128)(2,1)S(1)}, u32[]{:S(2)}, u32[]{:S(2)}) collective-permute-start(bf16[128,512]{1,0:T(8,128)(2,1)} %collective-permute-done.7), channel_id=1, source_target_pairs={{0,30},{2,0},{4,2},{6,4},{8,6},{10,8},{12,10},{14,12},{16,14},{18,... | collective-permute-start | bytes 393224 | tf_op jit(solution)/shard_map/ppermute | solution.py:26
  98.0 10.3 %collective-permute-start.10 = (bf16[128,512]{1,0:T(8,128)(2,1)}, bf16[128,512]{1,0:T(8,128)(2,1)}, u32[]{:S(2)}, u32[]{:S(2)}) collective-permute-start(bf16[128,512]{1,0:T(8,128)(2,1)} %collective-permute-done.8), channel_id=1, source_target_pairs={{0,2},{2,4},{4,6},{6,8},{8,10},{10,12},{12,14},{14,16},{16,18},{18... | collective-permute-start | bytes 393224 | tf_op jit(solution)/shard_map/ppermute | solution.py:23
  100.2 9.9 %collective-permute-start.11 = (bf16[128,512]{1,0:T(8,128)(2,1)S(1)}, bf16[128,512]{1,0:T(8,128)(2,1)}, u32[]{:S(2)}, u32[]{:S(2)}) collective-permute-start(bf16[128,512]{1,0:T(8,128)(2,1)S(1)} %collective-permute-done.9), channel_id=1, source_target_pairs={{0,30},{2,0},{4,2},{6,4},{8,6},{10,8},{12,10},{14,12},{16,14},{18,... | collective-permute-start | bytes 393224 | tf_op jit(solution)/shard_map/ppermute | solution.py:26
  109.3 10.7 %collective-permute-start.12 = (bf16[128,512]{1,0:T(8,128)(2,1)}, bf16[128,512]{1,0:T(8,128)(2,1)}, u32[]{:S(2)}, u32[]{:S(2)}) collective-permute-start(bf16[128,512]{1,0:T(8,128)(2,1)} %collective-permute-done.10), channel_id=1, source_target_pairs={{0,2},{2,4},{4,6},{6,8},{8,10},{10,12},{12,14},{14,16},{16,18},{18... | collective-permute-start | bytes 393224 | tf_op jit(solution)/shard_map/ppermute | solution.py:23
  109.4 33.7 %collective-permute-start.18 = (bf16[64,4,8,128]{3,2,1,0:T(8,128)(2,1)}, bf16[64,4,8,128]{3,2,1,0:T(8,128)(2,1)}, u32[]{:S(2)}, u32[]{:S(2)}) collective-permute-start(bf16[64,4,8,128]{3,2,1,0:T(8,128)(2,1)} %collective-permute-done.17), channel_id=1, source_target_pairs={{0,16},{2,18},{4,20},{6,22},{8,24},{10,26},{12,28},{14,30},{16,0},... | collective-permute-start | bytes 1572872 | tf_op jit(solution)/shard_map/ppermute | solution.py:36
  111.1 18.9 %collective-permute-start.13 = (bf16[128,512]{1,0:T(8,128)(2,1)}, bf16[128,512]{1,0:T(8,128)(2,1)S(1)}, u32[]{:S(2)}, u32[]{:S(2)}) collective-permute-start(bf16[128,512]{1,0:T(8,128)(2,1)} %collective-permute-done.11), channel_id=1, source_target_pairs={{0,30},{2,0},{4,2},{6,4},{8,6},{10,8},{12,10},{14,12},{16,14},{18,... | collective-permute-start | bytes 393224 | tf_op jit(solution)/shard_map/ppermute | solution.py:26
  121.0 14.7 %collective-permute-start.14 = (bf16[128,512]{1,0:T(8,128)(2,1)}, bf16[128,512]{1,0:T(8,128)(2,1)}, u32[]{:S(2)}, u32[]{:S(2)}) collective-permute-start(bf16[128,512]{1,0:T(8,128)(2,1)} %collective-permute-done.12), channel_id=1, source_target_pairs={{0,2},{2,4},{4,6},{6,8},{8,10},{10,12},{12,14},{14,16},{16,18},{18... | collective-permute-start | bytes 393224 | tf_op jit(solution)/shard_map/ppermute | solution.py:23
  335.9 83.9 %collective-permute-start.19 = (bf16[4,8,64,128]{3,2,1,0:T(8,128)(2,1)S(1)}, bf16[4,8,64,128]{3,2,1,0:T(8,128)(2,1)}, u32[]{:S(2)}, u32[]{:S(2)}) collective-permute-start(bf16[4,8,64,128]{3,2,1,0:T(8,128)(2,1)S(1)} %divide_convert_fusion), channel_id=1, source_target_pairs={{0,2},{2,0},{4,6},{6,4},{8,10},{10,8},{12,14},{14,12},{16,18},{18,... | collective-permute-start | bytes 1572872 | tf_op jit(solution)/shard_map/ppermute | solution.py:36
  419.8 14.4 %collective-permute-start.20 = (bf16[4,8,64,128]{3,2,1,0:T(8,128)(2,1)}, bf16[4,8,64,128]{3,2,1,0:T(8,128)(2,1)S(1)}, u32[]{:S(2)}, u32[]{:S(2)}) collective-permute-start(bf16[4,8,64,128]{3,2,1,0:T(8,128)(2,1)} %collective-permute-done.19), channel_id=1, source_target_pairs={{0,4},{2,6},{4,0},{6,2},{8,12},{10,14},{12,8},{14,10},{16,20},{18,... | collective-permute-start | bytes 1572872 | tf_op jit(solution)/shard_map/ppermute | solution.py:36
  434.3 13.4 %collective-permute-start.21 = (bf16[4,8,64,128]{3,2,1,0:T(8,128)(2,1)S(1)}, bf16[4,8,64,128]{3,2,1,0:T(8,128)(2,1)S(1)}, u32[]{:S(2)}, u32[]{:S(2)}) collective-permute-start(bf16[4,8,64,128]{3,2,1,0:T(8,128)(2,1)S(1)} %collective-permute-done.20), channel_id=1, source_target_pairs={{0,8},{2,10},{4,12},{6,14},{8,0},{10,2},{12,4},{14,6},{16,24},{18,... | collective-permute-start | bytes 1572872 | tf_op jit(solution)/shard_map/ppermute | solution.py:36
  447.7 24.6 %collective-permute-start.22 = (bf16[4,8,64,128]{3,2,1,0:T(8,128)(2,1)S(1)}, bf16[4,8,64,128]{3,2,1,0:T(8,128)(2,1)S(1)}, u32[]{:S(2)}, u32[]{:S(2)}) collective-permute-start(bf16[4,8,64,128]{3,2,1,0:T(8,128)(2,1)S(1)} %collective-permute-done.21), channel_id=1, source_target_pairs={{0,16},{2,18},{4,20},{6,22},{8,24},{10,26},{12,28},{14,30},{16,0},... | collective-permute-start | bytes 1572872 | tf_op jit(solution)/shard_map/ppermute | solution.py:36
  449.0 24.3 %copy-start.2 = (f32[4,8,128,128]{3,2,1,0:T(8,128)S(1)}, f32[4,8,128,128]{3,2,1,0:T(8,128)}, u32[]{:S(2)}) copy-start(f32[4,8,128,128]{3,2,1,0:T(8,128)} %custom-call) | copy-start | bytes 6291460
  540.5 267.6 %all-reduce.3.cloned.1.call-start = ((), (), s32[]{:S(2)}) async-start(), calls=%async_computation.1 | async-start | bytes 2097152 | tf_op jit(solution)/shard_map/psum | solution.py:317
  541.0 26.8 %copy-start.11 = (f32[4,8,192,64]{3,2,1,0:T(8,128)S(1)}, f32[4,8,192,64]{3,2,1,0:T(8,128)}, u32[]{:S(2)}) copy-start(f32[4,8,192,64]{3,2,1,0:T(8,128)} %copy-done.10) | copy-start | bytes 4718596
  665.2 38.6 %copy-start.21 = (bf16[128,512]{0,1:T(8,128)(2,1)S(1)}, bf16[128,512]{0,1:T(8,128)(2,1)}, u32[]{:S(2)}) copy-start(bf16[128,512]{0,1:T(8,128)(2,1)} %copy-done.20) | copy-start | bytes 393220
  757.3 53.0 %copy-start.1 = (bf16[32,128,64]{1,2,0:T(8,128)(2,1)S(1)}, bf16[32,128,64]{1,2,0:T(8,128)(2,1)}, u32[]{:S(2)}) copy-start(bf16[32,128,64]{1,2,0:T(8,128)(2,1)} %param.21) | copy-start | bytes 1572868
  (33 other events, 162.0 us)
Sparse Core Ops, SparseCore 0:
  10.2 49.6 all-gather.7
  62.0 150.8 all-gather.9
  540.6 124.5 all-gather.11
  716.6 91.4 all-reduce.2
